TPU v7x, 32 devices: a whole 2x2x4 slice. The times are simulated.
32 devices in a mesh: seq: 8 (over z, x), tp: 4 (over y, core).
Axes of the slice: x: 2, y: 2, z: 4, core: 2. Of those that a mesh axis runs over, the one named last changes fastest.
Arguments:
- hidden_in: bfloat16 [16, 2048], replicated, may hold values from -6 to 6
- lengths: int32 [16], replicated, may hold values from 1 to 511, 2431 in all
- positions: int32 [16], replicated, may hold values from 0 to 1023
- query_weight: bfloat16 [2, 2048, 2048], P(None, 'seq', 'tp'), may hold values from -0.125 to 0.125
- key_weight: bfloat16 [2, 2048, 512], P(None, 'seq', 'tp'), may hold values from -4 to 4
- value_weight: bfloat16 [2, 2048, 512], P(None, 'seq', 'tp'), may hold values from -0.125 to 0.125
- out_weight: bfloat16 [2, 2048, 2048], P(None, 'tp', 'seq'), may hold values from -0.125 to 0.125
- gate_weight: bfloat16 [2, 2048, 8192], P(None, 'seq', 'tp'), may hold values from -0.125 to 0.125
- up_weight: bfloat16 [2, 2048, 8192], P(None, 'seq', 'tp'), may hold values from -0.125 to 0.125
- down_weight: bfloat16 [2, 8192, 2048], P(None, 'tp', 'seq'), may hold values from -0.0625 to 0.0625
- key_cache: bfloat16 [2, 16, 512, 512], P(None, None, 'seq', 'tp'), may hold values from -80 to 80
- value_cache: bfloat16 [2, 16, 512, 512], P(None, None, 'seq', 'tp'), may hold values from -6 to 6
Outputs:
- hidden_out: bfloat16 [16, 2048], replicated
- key_out: bfloat16 [2, 16, 512, 512], P(None, None, 'seq', 'tp')
- value_out: bfloat16 [2, 16, 512, 512], P(None, None, 'seq', 'tp')
Inputs may be any that keep to these rules, and one draw needn't show every extreme that they name: Request b has its cached rows at positions 0 .. lengths[b] - 1 and its new token goes to row lengths[b]; rows above are padding. The longest request has exactly 511 cached rows.
All inputs are finite; a program needn't handle non-finite values.
Results may differ from a plain program's by a relative error of at most 0.015.
Values may be sent and summed in bfloat16 or wider, within the bound.
No kernel may reach another device: no remote copies, remote signals or barrier semaphores. Data moves between devices by JAX's collectives and lax.ppermute only.
A program may use at most 64 MiB of HBM per device.

v0:
```python
import math
import jax
import jax.numpy as jnp
from jax import lax
from jax.sharding import PartitionSpec as P

HEAD_DIM = 64
LAYERS = 2
eps_norm = 1e-05
neg_fill = -1e30


def rms_norm(stream):
    as_float = stream.astype(jnp.float32)
    spread = jnp.mean(as_float * as_float, axis=-1, keepdims=True)
    return (as_float * lax.rsqrt(spread + eps_norm)).astype(jnp.bfloat16)


def rotate(heads, positions):
    half_dim = heads.shape[-1] // 2
    inverse = 500000.0 ** (-(2.0 * jnp.arange(half_dim, dtype=jnp.float32)) / heads.shape[-1])
    angles = positions.astype(jnp.float32)[:, None] * inverse[None, :]
    cosine = jnp.cos(angles)[:, None, :]
    sine = jnp.sin(angles)[:, None, :]
    first_half = heads[..., :half_dim]
    second_half = heads[..., half_dim:]
    return jnp.concatenate(
        [first_half * cosine - second_half * sine, second_half * cosine + first_half * sine],
        axis=-1,
    )


def per_device(
    hidden_in,
    lengths,
    positions,
    query_weight,
    key_weight,
    value_weight,
    out_weight,
    gate_weight,
    up_weight,
    down_weight,
    key_cache,
    value_cache,
):
    seq_index = lax.axis_index("seq")
    row_count = query_weight.shape[1]
    row_start = seq_index * row_count
    col_count = out_weight.shape[2]
    col_start = seq_index * col_count
    block_len = key_cache.shape[2]
    kv_width_here = key_cache.shape[3]
    query_width = query_weight.shape[2]
    requests = hidden_in.shape[0]
    group_heads = query_width // HEAD_DIM
    kv_here = kv_width_here // HEAD_DIM
    repeat = group_heads // kv_here
    score_scale = 1.0 / math.sqrt(HEAD_DIM)
    global_slots = seq_index * block_len + jnp.arange(block_len, dtype=jnp.int32)
    new_slot = (global_slots[None, :] == lengths[:, None])[:, :, None]
    live_mask = (global_slots[None, :] <= lengths[:, None])[:, None, None, :]

    def finish(part_terms, stream_now):
        summed = lax.psum(part_terms, "tp")
        own_cols = lax.dynamic_slice_in_dim(stream_now, col_start, col_count, 1).astype(jnp.float32)
        return lax.all_gather((own_cols + summed).astype(jnp.bfloat16), "seq", axis=1, tiled=True)

    stream = hidden_in
    key_layers = []
    value_layers = []
    for layer_idx in range(LAYERS):
        normed = rms_norm(stream)
        own_rows = lax.dynamic_slice_in_dim(normed, row_start, row_count, 1)
        query_part = jnp.dot(own_rows, query_weight[layer_idx], preferred_element_type=jnp.float32)
        key_part = jnp.dot(own_rows, key_weight[layer_idx], preferred_element_type=jnp.float32)
        value_part = jnp.dot(own_rows, value_weight[layer_idx], preferred_element_type=jnp.float32)
        query, key_new, value_new = lax.psum((query_part, key_part, value_part), "seq")
        query = rotate(query.reshape(requests, group_heads, HEAD_DIM), positions).astype(
            jnp.bfloat16
        )
        query = query.reshape(requests, kv_here, repeat, HEAD_DIM)
        key_new = (
            rotate(key_new.reshape(requests, kv_here, HEAD_DIM), positions)
            .astype(jnp.bfloat16)
            .reshape(requests, kv_width_here)
        )
        value_new = value_new.astype(jnp.bfloat16)
        key_rows = jnp.where(new_slot, key_new[:, None, :], key_cache[layer_idx])
        value_rows = jnp.where(new_slot, value_new[:, None, :], value_cache[layer_idx])
        key_heads = key_rows.reshape(requests, block_len, kv_here, HEAD_DIM)
        value_heads = value_rows.reshape(requests, block_len, kv_here, HEAD_DIM)
        scores = (
            jnp.einsum("bkrd,bskd->bkrs", query, key_heads, preferred_element_type=jnp.float32)
            * score_scale
        )
        scores = jnp.where(live_mask, scores, neg_fill)
        row_top = lax.pmax(jnp.max(scores, axis=3), "seq")
        weights = jnp.where(live_mask, jnp.exp(scores - row_top[..., None]), 0.0)
        local_sums = jnp.sum(weights, axis=3)
        local_acc = jnp.einsum(
            "bkrs,bskd->bkrd",
            weights.astype(jnp.bfloat16),
            value_heads,
            preferred_element_type=jnp.float32,
        )
        totals, weighted = lax.psum((local_sums, local_acc), "seq")
        attended = (
            (weighted / totals[..., None]).astype(jnp.bfloat16).reshape(requests, query_width)
        )
        attn_terms = jnp.dot(attended, out_weight[layer_idx], preferred_element_type=jnp.float32)
        mid = finish(attn_terms, stream)
        normed_two = rms_norm(mid)
        rows_two = lax.dynamic_slice_in_dim(normed_two, row_start, row_count, 1)
        gate_part = jnp.dot(rows_two, gate_weight[layer_idx], preferred_element_type=jnp.float32)
        up_part = jnp.dot(rows_two, up_weight[layer_idx], preferred_element_type=jnp.float32)
        gate_sum, up_sum = lax.psum((gate_part, up_part), "seq")
        hidden = (jax.nn.silu(gate_sum) * up_sum).astype(jnp.bfloat16)
        down_terms = jnp.dot(hidden, down_weight[layer_idx], preferred_element_type=jnp.float32)
        stream = finish(down_terms, mid)
        key_layers.append(key_rows)
        value_layers.append(value_rows)
    return (stream, jnp.stack(key_layers), jnp.stack(value_layers))


def solution(mesh):
    return jax.shard_map(
        per_device,
        mesh=mesh,
        in_specs=(
            P(),
            P(),
            P(),
            P(None, "seq", "tp"),
            P(None, "seq", "tp"),
            P(None, "seq", "tp"),
            P(None, "tp", "seq"),
            P(None, "seq", "tp"),
            P(None, "seq", "tp"),
            P(None, "tp", "seq"),
            P(None, None, "seq", "tp"),
            P(None, None, "seq", "tp"),
        ),
        out_specs=(P(), P(None, None, "seq", "tp"), P(None, None, "seq", "tp")),
        check_vma=False,
    )
```

profile of v0, /device:TPU:0, one launch (start us, length us, event | category | flops | bytes accessed | tf_op | source)
XLA Modules:
  0.0 562.6 jit_solution(6855281874656980006)
XLA Ops:
  7.2 0.9 convert_element_type.105
  8.1 1.0 multiply_reduce_fusion.3
  9.1 1.0 fusion.46
  10.2 1.0 fusion.48
  11.3 1.1 fusion.32
  12.5 1.0 slice.86
  13.5 0.2 squeeze.58
  13.7 39.8 %all-reduce.3 = (bf16[16,128]{1,0:T(8,128)(2,1)S(1)}, f32[16,2,64]{2,1,0:T(2,128)S(1)}, f32[16,8,64]{2,1,0:T(8,128)S(1)}) all-reduce(f32[16,128]{1,0:T(8,128)S(1)} %fusion.46, f32[16,2,64]{2,1,0:T(2,128)S(1)} %reshape.206, f32[16,8,64]{2,1,0:T(8,128)S(1)} %reshape.205), channel_id=1, replica_groups=mesh['seq'=8,'tp'=4] {'seq'}, use_global_device_ids=true, to_apply=%region_5.6 | all-reduce | flops 12288 | bytes 94208 | tf_op jit(solution)/shard_map/psum | solution.py:78
  53.6 0.7 broadcast_in_dim.117
  54.3 1.1 squeeze.56
  55.3 0.1 multiply_cosine_fusion
  55.4 0.1 multiply_subtract_fusion.1
  55.5 0.1 subtract_convert_fusion.1
  55.8 1.7 fusion.88
  57.5 33.0 %pmax.14 = f32[16,2,4]{2,1,0:T(2,128)S(1)} all-reduce(f32[16,2,4]{2,1,0:T(2,128)S(1)} %get-tuple-element.38), channel_id=1, replica_groups=mesh['seq'=8,'tp'=4] {'seq'}, use_global_device_ids=true, to_apply=%region_4.5 | all-reduce | flops 128 | bytes 1024 | tf_op jit(solution)/shard_map/pmax | solution.py:98
  90.5 0.2 fusion.56
  90.7 1.0 fusion.21
  91.8 33.8 %all-reduce.2 = (f32[16,2,4,64]{3,2,1,0:T(4,128)S(1)}, f32[16,2,4]{2,1,0:T(2,128)S(1)}) all-reduce(f32[16,2,4,64]{3,2,1,0:T(4,128)S(1)} %fusion.21, f32[16,2,4]{2,1,0:T(2,128)S(1)} %fusion.56), channel_id=1, replica_groups=mesh['seq'=8,'tp'=4] {'seq'}, use_global_device_ids=true, to_apply=%region_6.7 | all-reduce | flops 8320 | bytes 66560 | tf_op jit(solution)/shard_map/psum | solution.py:107
  125.6 0.1 divide_convert_fusion.1
  125.7 0.1 reshape.207
  125.9 0.1 fusion.30
  126.0 10.1 %psum.131 = f32[16,256]{1,0:T(8,128)S(1)} all-reduce(f32[16,256]{1,0:T(8,128)S(1)} %fusion.30), channel_id=1, replica_groups=mesh['seq'=8,'tp'=4] {'tp'}, use_global_device_ids=true, to_apply=%region_9.10 | all-reduce | flops 4096 | bytes 32768 | tf_op jit(solution)/shard_map/psum | solution.py:65
  136.1 0.7 add_convert_fusion.5
  136.8 30.5 %all_gather.12 = bf16[16,2048]{1,0:T(8,128)(2,1)S(1)} all-gather(bf16[16,256]{1,0:T(8,128)(2,1)S(1)} %add_convert_fusion.5), channel_id=1, replica_groups=mesh['seq'=8,'tp'=4] {'seq'}, dimensions={1}, use_global_device_ids=true | all-gather | bytes 73728 | tf_op jit(solution)/shard_map/all_gather | solution.py:67
  167.3 0.1 multiply_reduce_fusion.2
  167.5 1.0 fusion.10
  168.4 2.3 fusion.12
  170.8 0.7 convert_element_type.131
  171.4 69.2 %all-reduce.11.cloned.1.call-done = (f32[16,2048]{1,0:T(8,128)}, f32[16,2048]{1,0:T(8,128)}) async-done(((f32[16,2048]{1,0:T(8,128)}, f32[16,2048]{1,0:T(8,128)}), (f32[16,2048]{1,0:T(8,128)}, f32[16,2048]{1,0:T(8,128)})) %all-reduce.11.cloned.1.call-update) | async-done | bytes 262160 | tf_op jit(solution)/shard_map/psum | solution.py:117
  240.6 1.6 fusion.8
  242.2 10.1 %psum.134 = f32[16,256]{1,0:T(8,128)S(1)} all-reduce(f32[16,256]{1,0:T(8,128)S(1)} %fusion.8), channel_id=1, replica_groups=mesh['seq'=8,'tp'=4] {'tp'}, use_global_device_ids=true, to_apply=%region_13.14 | all-reduce | flops 4096 | bytes 32768 | tf_op jit(solution)/shard_map/psum | solution.py:65
  252.3 30.5 %all_gather.13 = bf16[16,2048]{1,0:T(8,128)(2,1)S(1)} all-gather(bf16[16,256]{1,0:T(8,128)(2,1)S(1)} %add_convert_fusion.4), channel_id=1, replica_groups=mesh['seq'=8,'tp'=4] {'seq'}, dimensions={1}, use_global_device_ids=true | all-gather | bytes 73728 | tf_op jit(solution)/shard_map/all_gather | solution.py:67
  282.9 0.1 multiply_reduce_fusion.1
  283.0 1.0 fusion.42
  284.0 1.0 fusion.44
  285.1 1.1 fusion.28
  286.4 36.4 %all-reduce.1 = (bf16[16,128]{1,0:T(8,128)(2,1)S(1)}, f32[16,2,64]{2,1,0:T(2,128)S(1)}, f32[16,8,64]{2,1,0:T(8,128)S(1)}) all-reduce(f32[16,128]{1,0:T(8,128)S(1)} %fusion.42, f32[16,2,64]{2,1,0:T(2,128)S(1)} %reshape.209, f32[16,8,64]{2,1,0:T(8,128)S(1)} %reshape.208), channel_id=1, replica_groups=mesh['seq'=8,'tp'=4] {'seq'}, use_global_device_ids=true, to_apply=%region_19.20 | all-reduce | flops 12288 | bytes 94208 | tf_op jit(solution)/shard_map/psum | solution.py:78
  322.8 0.1 multiply_subtract_fusion
  322.9 0.1 maximum_convert_fusion.1
  323.0 0.7 convert_element_type.132
  323.7 0.7 broadcast_in_dim.120
  324.4 1.9 broadcast_select_fusion.1
  326.2 1.2 squeeze.67
  327.4 0.2 squeeze.65
  327.7 0.1 subtract_convert_fusion
  327.8 1.2 fusion.89
  329.0 33.0 %pmax.15 = f32[16,2,4]{2,1,0:T(2,128)S(1)} all-reduce(f32[16,2,4]{2,1,0:T(2,128)S(1)} %get-tuple-element.40), channel_id=1, replica_groups=mesh['seq'=8,'tp'=4] {'seq'}, use_global_device_ids=true, to_apply=%region_18.19 | all-reduce | flops 128 | bytes 1024 | tf_op jit(solution)/shard_map/pmax | solution.py:98
  362.0 0.9 fusion.58
  362.9 1.1 fusion.20
  364.0 34.0 %all-reduce = (f32[16,2,4,64]{3,2,1,0:T(4,128)S(1)}, f32[16,2,4]{2,1,0:T(2,128)S(1)}) all-reduce(f32[16,2,4,64]{3,2,1,0:T(4,128)S(1)} %fusion.20, f32[16,2,4]{2,1,0:T(2,128)S(1)} %fusion.58), channel_id=1, replica_groups=mesh['seq'=8,'tp'=4] {'seq'}, use_global_device_ids=true, to_apply=%region_20.21 | all-reduce | flops 8320 | bytes 66560 | tf_op jit(solution)/shard_map/psum | solution.py:107
  398.0 0.1 divide_convert_fusion
  398.1 0.1 reshape.210
  398.2 1.1 fusion.26
  399.3 10.1 %psum.140 = f32[16,256]{1,0:T(8,128)S(1)} all-reduce(f32[16,256]{1,0:T(8,128)S(1)} %fusion.26), channel_id=1, replica_groups=mesh['seq'=8,'tp'=4] {'tp'}, use_global_device_ids=true, to_apply=%region_23.24 | all-reduce | flops 4096 | bytes 32768 | tf_op jit(solution)/shard_map/psum | solution.py:65
  409.4 30.5 %all_gather.14 = bf16[16,2048]{1,0:T(8,128)(2,1)S(1)} all-gather(bf16[16,256]{1,0:T(8,128)(2,1)S(1)} %add_convert_fusion.3), channel_id=1, replica_groups=mesh['seq'=8,'tp'=4] {'seq'}, dimensions={1}, use_global_device_ids=true | all-gather | bytes 73728 | tf_op jit(solution)/shard_map/all_gather | solution.py:67
  439.9 0.1 multiply_reduce_fusion
  440.0 0.9 fusion.4
  441.0 2.3 fusion.6
  443.4 1.1 pad_maximum_fusion
  444.4 68.8 %all-reduce.9.cloned.1.call-done = (f32[16,2048]{1,0:T(8,128)}, f32[16,2048]{1,0:T(8,128)}) async-done(((f32[16,2048]{1,0:T(8,128)}, f32[16,2048]{1,0:T(8,128)}), (f32[16,2048]{1,0:T(8,128)}, f32[16,2048]{1,0:T(8,128)})) %all-reduce.9.cloned.1.call-update) | async-done | bytes 262160 | tf_op jit(solution)/shard_map/psum | solution.py:117
  513.3 1.2 fusion.2
  514.5 10.1 %psum.143 = f32[16,256]{1,0:T(8,128)S(1)} all-reduce(f32[16,256]{1,0:T(8,128)S(1)} %fusion.2), channel_id=1, replica_groups=mesh['seq'=8,'tp'=4] {'tp'}, use_global_device_ids=true, to_apply=%region_27.28 | all-reduce | flops 4096 | bytes 32768 | tf_op jit(solution)/shard_map/psum | solution.py:65
  524.6 30.5 %all_gather.15 = bf16[16,2048]{1,0:T(8,128)(2,1)S(1)} all-gather(bf16[16,256]{1,0:T(8,128)(2,1)S(1)} %add_convert_fusion.2), channel_id=1, replica_groups=mesh['seq'=8,'tp'=4] {'seq'}, dimensions={1}, use_global_device_ids=true | all-gather | bytes 73728 | tf_op jit(solution)/shard_map/all_gather | solution.py:67
  555.1 0.6 copy.36
  (57 shorter events, 0.8 us)
Async XLA Ops:
  7.2 47.1 %slice-start = ((bf16[2,16,64,128]{3,2,1,0:T(8,128)(2,1)}), bf16[1,16,64,128]{3,2,1,0:T(8,128)(2,1)S(1)}, s32[]{:S(2)}) async-start(bf16[2,16,64,128]{3,2,1,0:T(8,128)(2,1)} %param.22), calls=%async_computation.2 | async-start | bytes 524288 | tf_op jit(solution)/shard_map/slice | solution.py:89
  7.2 48.1 %copy-start.15 = (s32[16]{0:T(128)S(1)}, s32[16]{0:T(128)}, u32[]{:S(2)}) copy-start(s32[16]{0:T(128)} %param.14) | copy-start | bytes 196
  7.2 48.5 %copy-start.13 = (s32[16]{0:T(128)S(1)}, s32[16]{0:T(128)}, u32[]{:S(2)}) copy-start(s32[16]{0:T(128)} %param.13) | copy-start | bytes 196
  7.2 233.4 %all-reduce.11.cloned.1.call-start = ((), (), s32[]{:S(2)}) async-start(), calls=%async_computation.1 | async-start | bytes 524288 | tf_op jit(solution)/shard_map/psum | solution.py:117
  53.6 0.7 copy-start.10
  54.3 71.6 %copy-start.7 = (bf16[2,512,256]{2,1,0:T(8,128)(2,1)S(1)}, bf16[2,512,256]{2,1,0:T(8,128)(2,1)}, u32[]{:S(2)}) copy-start(bf16[2,512,256]{2,1,0:T(8,128)(2,1)} %param.18) | copy-start | bytes 1572868
  55.5 111.9 %copy-start = (bf16[2,256,2048]{2,1,0:T(8,128)(2,1)S(1)}, bf16[2,256,2048]{2,1,0:T(8,128)(2,1)}, u32[]{:S(2)}) copy-start(bf16[2,256,2048]{2,1,0:T(8,128)(2,1)} %param.20) | copy-start | bytes 6291460
  55.7 112.7 %copy-start.9 = (pred[16,64]{1,0:T(8,128)(4,1)}, pred[16,64]{1,0:T(8,128)(4,1)S(1)}, u32[]{:S(2)}) copy-start(pred[16,64]{1,0:T(8,128)(4,1)S(1)} %get-tuple-element.34) | copy-start | bytes 3076
  55.7 112.7 %copy-start.12 = (pred[16,64]{1,0:T(8,128)(4,1)}, pred[16,64]{1,0:T(8,128)(4,1)S(1)}, u32[]{:S(2)}) copy-start(pred[16,64]{1,0:T(8,128)(4,1)S(1)} %get-tuple-element.35) | copy-start | bytes 3076
  168.4 155.9 %copy-start.1 = (bf16[2,16,64,128]{3,2,1,0:T(8,128)(2,1)S(1)}, bf16[2,16,64,128]{3,2,1,0:T(8,128)(2,1)}, u32[]{:S(2)}) copy-start(bf16[2,16,64,128]{3,2,1,0:T(8,128)(2,1)} %param.23) | copy-start | bytes 1572868
  168.4 155.9 %copy-start.2 = (bf16[2,16,64,128]{3,2,1,0:T(8,128)(2,1)S(1)}, bf16[2,16,64,128]{3,2,1,0:T(8,128)(2,1)}, u32[]{:S(2)}) copy-start(bf16[2,16,64,128]{3,2,1,0:T(8,128)(2,1)} %param.22) | copy-start | bytes 1572868
  170.7 342.6 %all-reduce.9.cloned.1.call-start = ((), (), s32[]{:S(2)}) async-start(), calls=%async_computation | async-start | bytes 524288 | tf_op jit(solution)/shard_map/psum | solution.py:117
  322.8 0.9 copy-start.11
  323.0 0.7 copy-start.8
  364.0 79.4 %copy-start.3 = (bf16[1,16,64,128]{3,2,1,0:T(8,128)(2,1)S(1)}, bf16[1,16,64,128]{3,2,1,0:T(8,128)(2,1)}, u32[]{:S(2)}) copy-start(bf16[1,16,64,128]{3,2,1,0:T(8,128)(2,1)} %get-tuple-element.17) | copy-start | bytes 786436
  364.0 79.4 %copy-start.4 = (bf16[1,16,64,128]{3,2,1,0:T(8,128)(2,1)S(1)}, bf16[1,16,64,128]{3,2,1,0:T(8,128)(2,1)}, u32[]{:S(2)}) copy-start(bf16[1,16,64,128]{3,2,1,0:T(8,128)(2,1)} %get-tuple-element.18) | copy-start | bytes 786436
  364.0 79.4 %copy-start.5 = (bf16[1,16,64,128]{3,2,1,0:T(8,128)(2,1)S(1)}, bf16[1,16,64,128]{3,2,1,0:T(8,128)(2,1)}, u32[]{:S(2)}) copy-start(bf16[1,16,64,128]{3,2,1,0:T(8,128)(2,1)} %get-tuple-element.32) | copy-start | bytes 786436
  364.0 79.4 %copy-start.6 = (bf16[1,16,64,128]{3,2,1,0:T(8,128)(2,1)S(1)}, bf16[1,16,64,128]{3,2,1,0:T(8,128)(2,1)}, u32[]{:S(2)}) copy-start(bf16[1,16,64,128]{3,2,1,0:T(8,128)(2,1)} %get-tuple-element.33) | copy-start | bytes 786436
  441.0 72.3 %copy-start.14 = (bf16[2,2048,256]{2,1,0:T(8,128)(2,1)S(1)}, bf16[2,2048,256]{2,1,0:T(8,128)(2,1)}, u32[]{:S(2)}) copy-start(bf16[2,2048,256]{2,1,0:T(8,128)(2,1)} %param.21) | copy-start | bytes 6291460
Sparse Core Ops, SparseCore 0:
  170.8 69.7 all-reduce.10
  443.5 69.7 all-reduce.8
where the time goes:
time: 564 us; the launch traced here: 563 us
  blocking collectives  372 us (66%)
  waiting for transfers between devices  138 us (24%)
  matrix products  22 us (4%)
  between operations  14.4 us (3%)
  other arithmetic  8.02 us (1%)
  local copies, waits for them, and re-layouts  7.62 us (1%)
    psum x2, waiting for transfers between devices, per_device(): gate_sum, up_sum = lax.psum((gate_part, up_part), 'seq')  138 us
    all_gather x4, blocking collectives, finish(): lax.all_gather((own_cols + summed).astype(jnp.bfloat16), 'seq', axis=1, t...  122 us
    psum x2, blocking collectives, per_device(): lax.psum((query_part, key_part, value_part), 'seq')  76.3 us
    psum x2, blocking collectives, per_device(): totals, weighted = lax.psum((local_sums, local_acc), 'seq')  67.8 us
    pmax x2, blocking collectives, per_device(): row_top = lax.pmax(jnp.max(scores, axis=3), 'seq')  66 us
    psum x4, blocking collectives, finish(): summed = lax.psum(part_terms, 'tp')  40.5 us
  transfers between devices with their start and end apart: 2, of which 2 were waited for; matrix products, arithmetic and copies ran while one was open for 0% of the time, Pallas kernels for 0%

commit v1 on v0

--- a/solution.py
+++ b/solution.py
@@ -8,6 +8,22 @@
 LAYERS = 2
 eps_norm = 1e-05
 neg_fill = -1e30
+
+
+def ring_gather(x, axis, dim):
+    ways, here, step = (lax.axis_size(axis), lax.axis_index(axis), x.shape[dim])
+    lengths = [n * ways if d == dim else n for d, n in enumerate(x.shape)]
+    full = lax.dynamic_update_slice_in_dim(jnp.zeros(lengths, x.dtype), x, here * step, axis=dim)
+    going_up = going_down = x
+    for far in range(1, ways // 2 + 1):
+        going_up = lax.ppermute(going_up, axis, [(d, (d + 1) % ways) for d in range(ways)])
+        full = lax.dynamic_update_slice_in_dim(full, going_up, (here - far) % ways * step, axis=dim)
+        if 2 * far < ways:
+            going_down = lax.ppermute(going_down, axis, [(d, (d - 1) % ways) for d in range(ways)])
+            full = lax.dynamic_update_slice_in_dim(
+                full, going_down, (here + far) % ways * step, axis=dim
+            )
+    return full
 
 
 def rms_norm(stream):
@@ -64,7 +80,7 @@
     def finish(part_terms, stream_now):
         summed = lax.psum(part_terms, "tp")
         own_cols = lax.dynamic_slice_in_dim(stream_now, col_start, col_count, 1).astype(jnp.float32)
-        return lax.all_gather((own_cols + summed).astype(jnp.bfloat16), "seq", axis=1, tiled=True)
+        return ring_gather((own_cols + summed).astype(jnp.bfloat16), "seq", 1)
 
     stream = hidden_in
     key_layers = []

time: 564 us -> 540 us (0.957)
  blocking collectives: 372 us -> 250 us
  starting transfers between devices: 0.08 us -> 57.9 us
  waiting for transfers between devices: 138 us -> 179 us
    all_gather x4 -> x0, blocking collectives: 122 us -> none  [finish(): lax.all_gather((own_cols + summed).astype(jnp.bfloat16), 'seq', axis=1, t...]
    ppermute x0 -> x28, starting transfers between devices: none -> 57.9 us  [the longest x12 56.1 us: ring_gather(): lax.ppermute(going_down, axis, [(d, (d - 1) % ways) for d in range(ways)])]
    ppermute x0 -> x28, waiting for transfers between devices: none -> 42 us  [the longest x16 38.3 us: ring_gather(): lax.ppermute(going_up, axis, [(d, (d + 1) % ways) for d in range(ways)])]
  transfers between devices with their start and end apart: 2 -> 30, of which waited for: 2 -> 24; matrix products, arithmetic and copies ran while one was open for 0% -> 0% of each run, Pallas kernels for 0% -> 0%
where the time goes in v1:
time: 540 us; the launch traced here: 539 us
  blocking collectives  250 us (46%)
  waiting for transfers between devices  179 us (33%)
  starting transfers between devices  57.9 us (11%)
  matrix products  21.6 us (4%)
  between operations  14.5 us (3%)
  local copies, waits for them, and re-layouts  8.52 us (2%)
  other arithmetic  8.07 us (1%)
    psum x2, waiting for transfers between devices, per_device(): gate_sum, up_sum = lax.psum((gate_part, up_part), 'seq')  137 us
    psum x2, blocking collectives, per_device(): lax.psum((query_part, key_part, value_part), 'seq')  73.7 us
    pmax x2, blocking collectives, per_device(): row_top = lax.pmax(jnp.max(scores, axis=3), 'seq')  67.9 us
    psum x2, blocking collectives, per_device(): totals, weighted = lax.psum((local_sums, local_acc), 'seq')  67.7 us
    ppermute x12, starting transfers between devices, ring_gather(): lax.ppermute(going_down, axis, [(d, (d - 1) % ways) for d in range(ways)])  56.1 us
    psum x4, blocking collectives, finish(): summed = lax.psum(part_terms, 'tp')  40.5 us
    ppermute x16, waiting for transfers between devices, ring_gather(): lax.ppermute(going_up, axis, [(d, (d + 1) % ways) for d in range(ways)])  38.3 us
  transfers between devices with their start and end apart: 30, of which 24 were waited for; matrix products, arithmetic and copies ran while one was open for 0% of the time, Pallas kernels for 0%

profile of v1, /device:TPU:0, one launch (start us, length us, event | category | flops | bytes accessed | tf_op | source)
XLA Modules:
  0.0 538.9 jit_solution(11210561653272061348)
XLA Ops:
  7.2 0.9 convert_element_type.105
  8.1 1.0 multiply_reduce_fusion.3
  9.1 1.0 fusion.46
  10.2 1.0 fusion.48
  11.3 1.1 fusion.32
  12.5 1.0 slice.86
  13.7 39.8 %all-reduce.3 = (bf16[16,128]{1,0:T(8,128)(2,1)S(1)}, f32[16,2,64]{2,1,0:T(2,128)S(1)}, f32[16,8,64]{2,1,0:T(8,128)S(1)}) all-reduce(f32[16,128]{1,0:T(8,128)S(1)} %fusion.46, f32[16,2,64]{2,1,0:T(2,128)S(1)} %reshape.206, f32[16,8,64]{2,1,0:T(8,128)S(1)} %reshape.205), channel_id=1, replica_groups=mesh['seq'=8,'tp'=4] {'seq'}, use_global_device_ids=true, to_apply=%region_5.6 | all-reduce | flops 12288 | bytes 94208 | tf_op jit(solution)/shard_map/psum | solution.py:94
  54.3 1.1 squeeze.56
  55.8 1.7 fusion.88
  57.5 33.0 %pmax.14 = f32[16,2,4]{2,1,0:T(2,128)S(1)} all-reduce(f32[16,2,4]{2,1,0:T(2,128)S(1)} %get-tuple-element.46), channel_id=1, replica_groups=mesh['seq'=8,'tp'=4] {'seq'}, use_global_device_ids=true, to_apply=%region_4.5 | all-reduce | flops 128 | bytes 1024 | tf_op jit(solution)/shard_map/pmax | solution.py:114
  90.7 1.0 fusion.21
  91.8 33.8 %all-reduce.2 = (f32[16,2,4,64]{3,2,1,0:T(4,128)S(1)}, f32[16,2,4]{2,1,0:T(2,128)S(1)}) all-reduce(f32[16,2,4,64]{3,2,1,0:T(4,128)S(1)} %fusion.21, f32[16,2,4]{2,1,0:T(2,128)S(1)} %fusion.56), channel_id=1, replica_groups=mesh['seq'=8,'tp'=4] {'seq'}, use_global_device_ids=true, to_apply=%region_6.7 | all-reduce | flops 8320 | bytes 66560 | tf_op jit(solution)/shard_map/psum | solution.py:123
  126.0 10.1 %psum.131 = f32[16,256]{1,0:T(8,128)S(1)} all-reduce(f32[16,256]{1,0:T(8,128)S(1)} %fusion.30), channel_id=1, replica_groups=mesh['seq'=8,'tp'=4] {'tp'}, use_global_device_ids=true, to_apply=%region_9.10 | all-reduce | flops 4096 | bytes 32768 | tf_op jit(solution)/shard_map/psum | solution.py:81
  136.8 4.7 collective-permute-start.1
  141.6 1.6 collective-permute-done
  143.2 4.7 collective-permute-start.3
  147.9 1.6 collective-permute-done.2
  149.5 4.7 collective-permute-start.5
  154.3 1.6 collective-permute-done.4
  155.9 6.3 %collective-permute-done.6 = bf16[16,256]{1,0:T(8,128)(2,1)S(1)} collective-permute-done((bf16[16,256]{1,0:T(8,128)(2,1)S(1)}, bf16[16,256]{1,0:T(8,128)(2,1)S(1)}, u32[]{:S(2)}, u32[]{:S(2)}) %collective-permute-start.6) | collective-permute-done | bytes 8224 | tf_op jit(solution)/shard_map/ppermute | solution.py:19
  162.4 1.0 fusion.10
  163.4 2.3 fusion.12
  165.7 68.3 %all-reduce.11.cloned.1.call-done = (f32[16,2048]{1,0:T(8,128)}, f32[16,2048]{1,0:T(8,128)}) async-done(((f32[16,2048]{1,0:T(8,128)}, f32[16,2048]{1,0:T(8,128)}), (f32[16,2048]{1,0:T(8,128)}, f32[16,2048]{1,0:T(8,128)})) %all-reduce.11.cloned.1.call-update) | async-done | bytes 262160 | tf_op jit(solution)/shard_map/psum | solution.py:133
  234.0 1.6 fusion.8
  235.6 10.1 %psum.134 = f32[16,256]{1,0:T(8,128)S(1)} all-reduce(f32[16,256]{1,0:T(8,128)S(1)} %fusion.8), channel_id=1, replica_groups=mesh['seq'=8,'tp'=4] {'tp'}, use_global_device_ids=true, to_apply=%region_13.14 | all-reduce | flops 4096 | bytes 32768 | tf_op jit(solution)/shard_map/psum | solution.py:81
  245.7 0.8 collective-permute-start.7
  247.2 3.9 collective-permute-start.8
  251.2 0.9 collective-permute-done.7
  252.6 5.0 collective-permute-start.10
  257.5 0.9 collective-permute-done.9
  258.9 5.0 collective-permute-start.12
  263.9 0.9 collective-permute-done.11
  265.3 5.9 %collective-permute-done.13 = bf16[16,256]{1,0:T(8,128)(2,1)S(1)} collective-permute-done((bf16[16,256]{1,0:T(8,128)(2,1)S(1)}, bf16[16,256]{1,0:T(8,128)(2,1)S(1)}, u32[]{:S(2)}, u32[]{:S(2)}) %collective-permute-start.13) | collective-permute-done | bytes 8224 | tf_op jit(solution)/shard_map/ppermute | solution.py:19
  271.3 1.0 fusion.42
  272.4 1.0 fusion.44
  273.4 1.1 fusion.28
  274.7 33.9 %all-reduce.1 = (bf16[16,128]{1,0:T(8,128)(2,1)S(1)}, f32[16,2,64]{2,1,0:T(2,128)S(1)}, f32[16,8,64]{2,1,0:T(8,128)S(1)}) all-reduce(f32[16,128]{1,0:T(8,128)S(1)} %fusion.42, f32[16,2,64]{2,1,0:T(2,128)S(1)} %reshape.209, f32[16,8,64]{2,1,0:T(8,128)S(1)} %reshape.208), channel_id=1, replica_groups=mesh['seq'=8,'tp'=4] {'seq'}, use_global_device_ids=true, to_apply=%region_19.20 | all-reduce | flops 12288 | bytes 94208 | tf_op jit(solution)/shard_map/psum | solution.py:94
  310.1 1.9 broadcast_select_fusion.1
  312.1 1.2 squeeze.67
  313.3 1.1 squeeze.65
  314.4 1.6 fusion.89
  316.0 34.9 %pmax.15 = f32[16,2,4]{2,1,0:T(2,128)S(1)} all-reduce(f32[16,2,4]{2,1,0:T(2,128)S(1)} %get-tuple-element.48), channel_id=1, replica_groups=mesh['seq'=8,'tp'=4] {'seq'}, use_global_device_ids=true, to_apply=%region_18.19 | all-reduce | flops 128 | bytes 1024 | tf_op jit(solution)/shard_map/pmax | solution.py:114
  350.9 0.9 fusion.58
  351.8 1.1 fusion.20
  352.9 33.8 %all-reduce = (f32[16,2,4,64]{3,2,1,0:T(4,128)S(1)}, f32[16,2,4]{2,1,0:T(2,128)S(1)}) all-reduce(f32[16,2,4,64]{3,2,1,0:T(4,128)S(1)} %fusion.20, f32[16,2,4]{2,1,0:T(2,128)S(1)} %fusion.58), channel_id=1, replica_groups=mesh['seq'=8,'tp'=4] {'seq'}, use_global_device_ids=true, to_apply=%region_20.21 | all-reduce | flops 8320 | bytes 66560 | tf_op jit(solution)/shard_map/psum | solution.py:123
  387.1 10.1 %psum.140 = f32[16,256]{1,0:T(8,128)S(1)} all-reduce(f32[16,256]{1,0:T(8,128)S(1)} %fusion.26), channel_id=1, replica_groups=mesh['seq'=8,'tp'=4] {'tp'}, use_global_device_ids=true, to_apply=%region_23.24 | all-reduce | flops 4096 | bytes 32768 | tf_op jit(solution)/shard_map/psum | solution.py:81
  397.3 4.7 collective-permute-start.15
  402.0 1.6 collective-permute-done.14
  403.6 4.7 collective-permute-start.17
  408.4 1.6 collective-permute-done.16
  410.0 4.7 collective-permute-start.19
  414.7 1.6 collective-permute-done.18
  416.4 6.3 %collective-permute-done.20 = bf16[16,256]{1,0:T(8,128)(2,1)S(1)} collective-permute-done((bf16[16,256]{1,0:T(8,128)(2,1)S(1)}, bf16[16,256]{1,0:T(8,128)(2,1)S(1)}, u32[]{:S(2)}, u32[]{:S(2)}) %collective-permute-start.20) | collective-permute-done | bytes 8224 | tf_op jit(solution)/shard_map/ppermute | solution.py:19
  422.9 1.0 fusion.4
  423.8 2.2 fusion.6
  426.0 68.3 %all-reduce.9.cloned.1.call-done = (f32[16,2048]{1,0:T(8,128)}, f32[16,2048]{1,0:T(8,128)}) async-done(((f32[16,2048]{1,0:T(8,128)}, f32[16,2048]{1,0:T(8,128)}), (f32[16,2048]{1,0:T(8,128)}, f32[16,2048]{1,0:T(8,128)})) %all-reduce.9.cloned.1.call-update) | async-done | bytes 262160 | tf_op jit(solution)/shard_map/psum | solution.py:133
  494.3 1.6 fusion.2
  495.9 10.1 %psum.143 = f32[16,256]{1,0:T(8,128)S(1)} all-reduce(f32[16,256]{1,0:T(8,128)S(1)} %fusion.2), channel_id=1, replica_groups=mesh['seq'=8,'tp'=4] {'tp'}, use_global_device_ids=true, to_apply=%region_27.28 | all-reduce | flops 4096 | bytes 32768 | tf_op jit(solution)/shard_map/psum | solution.py:81
  506.0 0.8 collective-permute-start.21
  506.9 1.1 pad_maximum_fusion
  507.9 3.9 collective-permute-start.22
  513.2 5.0 collective-permute-start.24
  519.6 5.0 collective-permute-start.26
  525.9 5.5 %collective-permute-done.27 = bf16[16,256]{1,0:T(8,128)(2,1)S(1)} collective-permute-done((bf16[16,256]{1,0:T(8,128)(2,1)S(1)}, bf16[16,256]{1,0:T(8,128)(2,1)S(1)}, u32[]{:S(2)}, u32[]{:S(2)}) %collective-permute-start.27) | collective-permute-done | bytes 8224 | tf_op jit(solution)/shard_map/ppermute | solution.py:19
  (142 shorter events, 12.5 us)
Async XLA Ops:
  7.2 47.1 %slice-start = ((bf16[2,16,64,128]{3,2,1,0:T(8,128)(2,1)}), bf16[1,16,64,128]{3,2,1,0:T(8,128)(2,1)S(1)}, s32[]{:S(2)}) async-start(bf16[2,16,64,128]{3,2,1,0:T(8,128)(2,1)} %param.22), calls=%async_computation.2 | async-start | bytes 524288 | tf_op jit(solution)/shard_map/slice | solution.py:105
  7.2 48.1 %copy-start.16 = (s32[16]{0:T(128)S(1)}, s32[16]{0:T(128)}, u32[]{:S(2)}) copy-start(s32[16]{0:T(128)} %param.14) | copy-start | bytes 196
  7.2 48.4 %copy-start.15 = (s32[16]{0:T(128)S(1)}, s32[16]{0:T(128)}, u32[]{:S(2)}) copy-start(s32[16]{0:T(128)} %param.13) | copy-start | bytes 196
  7.2 226.8 %all-reduce.11.cloned.1.call-start = ((), (), s32[]{:S(2)}) async-start(), calls=%async_computation.1 | async-start | bytes 524288 | tf_op jit(solution)/shard_map/psum | solution.py:133
  53.6 0.7 copy-start.12
  54.2 71.6 %copy-start.7 = (bf16[2,512,256]{2,1,0:T(8,128)(2,1)S(1)}, bf16[2,512,256]{2,1,0:T(8,128)(2,1)}, u32[]{:S(2)}) copy-start(bf16[2,512,256]{2,1,0:T(8,128)(2,1)} %param.18) | copy-start | bytes 1572868
  55.7 106.5 %copy-start.11 = (pred[16,64]{1,0:T(8,128)(4,1)}, pred[16,64]{1,0:T(8,128)(4,1)S(1)}, u32[]{:S(2)}) copy-start(pred[16,64]{1,0:T(8,128)(4,1)S(1)} %get-tuple-element.42) | copy-start | bytes 3076
  55.7 106.5 %copy-start.14 = (pred[16,64]{1,0:T(8,128)(4,1)}, pred[16,64]{1,0:T(8,128)(4,1)S(1)}, u32[]{:S(2)}) copy-start(pred[16,64]{1,0:T(8,128)(4,1)S(1)} %get-tuple-element.43) | copy-start | bytes 3076
  55.8 106.6 %copy-start = (bf16[2,256,2048]{2,1,0:T(8,128)(2,1)S(1)}, bf16[2,256,2048]{2,1,0:T(8,128)(2,1)}, u32[]{:S(2)}) copy-start(bf16[2,256,2048]{2,1,0:T(8,128)(2,1)} %param.20) | copy-start | bytes 6291460
  136.8 6.3 %collective-permute-start = (bf16[16,256]{1,0:T(8,128)(2,1)S(1)}, bf16[16,256]{1,0:T(8,128)(2,1)S(1)}, u32[]{:S(2)}, u32[]{:S(2)}) collective-permute-start(bf16[16,256]{1,0:T(8,128)(2,1)S(1)} %get-tuple-element.24), channel_id=1, source_target_pairs={{0,4},{4,8},{8,12},{12,16},{16,20},{20,24},{24,28},{28,0},{1,5},{5... | collective-permute-start | bytes 24584 | tf_op jit(solution)/shard_map/ppermute | solution.py:19
  136.8 6.4 %collective-permute-start.1 = (bf16[16,256]{1,0:T(8,128)(2,1)S(1)}, bf16[16,256]{1,0:T(8,128)(2,1)S(1)}, u32[]{:S(2)}, u32[]{:S(2)}) collective-permute-start(bf16[16,256]{1,0:T(8,128)(2,1)S(1)} %get-tuple-element.24), channel_id=1, source_target_pairs={{0,28},{4,0},{8,4},{12,8},{16,12},{20,16},{24,20},{28,24},{1,29},{... | collective-permute-start | bytes 24584 | tf_op jit(solution)/shard_map/ppermute | solution.py:22
  143.2 6.3 %collective-permute-start.2 = (bf16[16,256]{1,0:T(8,128)(2,1)S(1)}, bf16[16,256]{1,0:T(8,128)(2,1)S(1)}, u32[]{:S(2)}, u32[]{:S(2)}) collective-permute-start(bf16[16,256]{1,0:T(8,128)(2,1)S(1)} %collective-permute-done), channel_id=1, source_target_pairs={{0,4},{4,8},{8,12},{12,16},{16,20},{20,24},{24,28},{28,0},{1,5},{5... | collective-permute-start | bytes 24584 | tf_op jit(solution)/shard_map/ppermute | solution.py:19
  143.2 6.3 %collective-permute-start.3 = (bf16[16,256]{1,0:T(8,128)(2,1)S(1)}, bf16[16,256]{1,0:T(8,128)(2,1)S(1)}, u32[]{:S(2)}, u32[]{:S(2)}) collective-permute-start(bf16[16,256]{1,0:T(8,128)(2,1)S(1)} %collective-permute-done.1), channel_id=1, source_target_pairs={{0,28},{4,0},{8,4},{12,8},{16,12},{20,16},{24,20},{28,24},{1,29},{... | collective-permute-start | bytes 24584 | tf_op jit(solution)/shard_map/ppermute | solution.py:22
  149.5 6.3 %collective-permute-start.4 = (bf16[16,256]{1,0:T(8,128)(2,1)S(1)}, bf16[16,256]{1,0:T(8,128)(2,1)S(1)}, u32[]{:S(2)}, u32[]{:S(2)}) collective-permute-start(bf16[16,256]{1,0:T(8,128)(2,1)S(1)} %collective-permute-done.2), channel_id=1, source_target_pairs={{0,4},{4,8},{8,12},{12,16},{16,20},{20,24},{24,28},{28,0},{1,5},{5... | collective-permute-start | bytes 24584 | tf_op jit(solution)/shard_map/ppermute | solution.py:19
  149.5 6.3 %collective-permute-start.5 = (bf16[16,256]{1,0:T(8,128)(2,1)S(1)}, bf16[16,256]{1,0:T(8,128)(2,1)S(1)}, u32[]{:S(2)}, u32[]{:S(2)}) collective-permute-start(bf16[16,256]{1,0:T(8,128)(2,1)S(1)} %collective-permute-done.3), channel_id=1, source_target_pairs={{0,28},{4,0},{8,4},{12,8},{16,12},{20,16},{24,20},{28,24},{1,29},{... | collective-permute-start | bytes 24584 | tf_op jit(solution)/shard_map/ppermute | solution.py:22
  155.9 6.3 %collective-permute-start.6 = (bf16[16,256]{1,0:T(8,128)(2,1)S(1)}, bf16[16,256]{1,0:T(8,128)(2,1)S(1)}, u32[]{:S(2)}, u32[]{:S(2)}) collective-permute-start(bf16[16,256]{1,0:T(8,128)(2,1)S(1)} %collective-permute-done.4), channel_id=1, source_target_pairs={{0,4},{4,8},{8,12},{12,16},{16,20},{20,24},{24,28},{28,0},{1,5},{5... | collective-permute-start | bytes 24584 | tf_op jit(solution)/shard_map/ppermute | solution.py:19
  163.4 146.8 %copy-start.1 = (bf16[2,16,64,128]{3,2,1,0:T(8,128)(2,1)S(1)}, bf16[2,16,64,128]{3,2,1,0:T(8,128)(2,1)}, u32[]{:S(2)}) copy-start(bf16[2,16,64,128]{3,2,1,0:T(8,128)(2,1)} %param.23) | copy-start | bytes 1572868
  163.4 146.8 %copy-start.2 = (bf16[2,16,64,128]{3,2,1,0:T(8,128)(2,1)S(1)}, bf16[2,16,64,128]{3,2,1,0:T(8,128)(2,1)}, u32[]{:S(2)}) copy-start(bf16[2,16,64,128]{3,2,1,0:T(8,128)(2,1)} %param.22) | copy-start | bytes 1572868
  165.6 328.6 %all-reduce.9.cloned.1.call-start = ((), (), s32[]{:S(2)}) async-start(), calls=%async_computation | async-start | bytes 524288 | tf_op jit(solution)/shard_map/psum | solution.py:133
  245.7 6.4 %collective-permute-start.7 = (bf16[16,256]{1,0:T(8,128)(2,1)S(1)}, bf16[16,256]{1,0:T(8,128)(2,1)S(1)}, u32[]{:S(2)}, u32[]{:S(2)}) collective-permute-start(bf16[16,256]{1,0:T(8,128)(2,1)S(1)} %get-tuple-element.22), channel_id=1, source_target_pairs={{0,4},{4,8},{8,12},{12,16},{16,20},{20,24},{24,28},{28,0},{1,5},{5... | collective-permute-start | bytes 24584 | tf_op jit(solution)/shard_map/ppermute | solution.py:19
  247.2 5.3 collective-permute-start.8
  252.1 6.3 %collective-permute-start.9 = (bf16[16,256]{1,0:T(8,128)(2,1)S(1)}, bf16[16,256]{1,0:T(8,128)(2,1)S(1)}, u32[]{:S(2)}, u32[]{:S(2)}) collective-permute-start(bf16[16,256]{1,0:T(8,128)(2,1)S(1)} %collective-permute-done.7), channel_id=1, source_target_pairs={{0,4},{4,8},{8,12},{12,16},{16,20},{20,24},{24,28},{28,0},{1,5},{5... | collective-permute-start | bytes 24584 | tf_op jit(solution)/shard_map/ppermute | solution.py:19
  252.6 6.3 %collective-permute-start.10 = (bf16[16,256]{1,0:T(8,128)(2,1)S(1)}, bf16[16,256]{1,0:T(8,128)(2,1)S(1)}, u32[]{:S(2)}, u32[]{:S(2)}) collective-permute-start(bf16[16,256]{1,0:T(8,128)(2,1)S(1)} %collective-permute-done.8), channel_id=1, source_target_pairs={{0,28},{4,0},{8,4},{12,8},{16,12},{20,16},{24,20},{28,24},{1,29},{... | collective-permute-start | bytes 24584 | tf_op jit(solution)/shard_map/ppermute | solution.py:22
  258.5 6.3 %collective-permute-start.11 = (bf16[16,256]{1,0:T(8,128)(2,1)S(1)}, bf16[16,256]{1,0:T(8,128)(2,1)S(1)}, u32[]{:S(2)}, u32[]{:S(2)}) collective-permute-start(bf16[16,256]{1,0:T(8,128)(2,1)S(1)} %collective-permute-done.9), channel_id=1, source_target_pairs={{0,4},{4,8},{8,12},{12,16},{16,20},{20,24},{24,28},{28,0},{1,5},{5... | collective-permute-start | bytes 24584 | tf_op jit(solution)/shard_map/ppermute | solution.py:19
  258.9 6.3 %collective-permute-start.12 = (bf16[16,256]{1,0:T(8,128)(2,1)S(1)}, bf16[16,256]{1,0:T(8,128)(2,1)S(1)}, u32[]{:S(2)}, u32[]{:S(2)}) collective-permute-start(bf16[16,256]{1,0:T(8,128)(2,1)S(1)} %collective-permute-done.10), channel_id=1, source_target_pairs={{0,28},{4,0},{8,4},{12,8},{16,12},{20,16},{24,20},{28,24},{1,29},{... | collective-permute-start | bytes 24584 | tf_op jit(solution)/shard_map/ppermute | solution.py:22
  264.8 6.3 %collective-permute-start.13 = (bf16[16,256]{1,0:T(8,128)(2,1)S(1)}, bf16[16,256]{1,0:T(8,128)(2,1)S(1)}, u32[]{:S(2)}, u32[]{:S(2)}) collective-permute-start(bf16[16,256]{1,0:T(8,128)(2,1)S(1)} %collective-permute-done.11), channel_id=1, source_target_pairs={{0,4},{4,8},{8,12},{12,16},{16,20},{20,24},{24,28},{28,0},{1,5},{5... | collective-permute-start | bytes 24584 | tf_op jit(solution)/shard_map/ppermute | solution.py:19
  308.6 0.9 copy-start.13
  308.8 0.7 copy-start.10
  313.3 73.7 %copy-start.8 = (bf16[2,512,256]{2,1,0:T(8,128)(2,1)S(1)}, bf16[2,512,256]{2,1,0:T(8,128)(2,1)}, u32[]{:S(2)}) copy-start(bf16[2,512,256]{2,1,0:T(8,128)(2,1)} %param.18) | copy-start | bytes 1572868
  397.2 6.4 %collective-permute-start.14 = (bf16[16,256]{1,0:T(8,128)(2,1)S(1)}, bf16[16,256]{1,0:T(8,128)(2,1)S(1)}, u32[]{:S(2)}, u32[]{:S(2)}) collective-permute-start(bf16[16,256]{1,0:T(8,128)(2,1)S(1)} %get-tuple-element.20), channel_id=1, source_target_pairs={{0,4},{4,8},{8,12},{12,16},{16,20},{20,24},{24,28},{28,0},{1,5},{5... | collective-permute-start | bytes 24584 | tf_op jit(solution)/shard_map/ppermute | solution.py:19
  397.3 6.3 %collective-permute-start.15 = (bf16[16,256]{1,0:T(8,128)(2,1)S(1)}, bf16[16,256]{1,0:T(8,128)(2,1)S(1)}, u32[]{:S(2)}, u32[]{:S(2)}) collective-permute-start(bf16[16,256]{1,0:T(8,128)(2,1)S(1)} %get-tuple-element.20), channel_id=1, source_target_pairs={{0,28},{4,0},{8,4},{12,8},{16,12},{20,16},{24,20},{28,24},{1,29},{... | collective-permute-start | bytes 24584 | tf_op jit(solution)/shard_map/ppermute | solution.py:22
  403.6 6.3 %collective-permute-start.16 = (bf16[16,256]{1,0:T(8,128)(2,1)S(1)}, bf16[16,256]{1,0:T(8,128)(2,1)S(1)}, u32[]{:S(2)}, u32[]{:S(2)}) collective-permute-start(bf16[16,256]{1,0:T(8,128)(2,1)S(1)} %collective-permute-done.14), channel_id=1, source_target_pairs={{0,4},{4,8},{8,12},{12,16},{16,20},{20,24},{24,28},{28,0},{1,5},{5... | collective-permute-start | bytes 24584 | tf_op jit(solution)/shard_map/ppermute | solution.py:19
  403.6 6.3 %collective-permute-start.17 = (bf16[16,256]{1,0:T(8,128)(2,1)S(1)}, bf16[16,256]{1,0:T(8,128)(2,1)S(1)}, u32[]{:S(2)}, u32[]{:S(2)}) collective-permute-start(bf16[16,256]{1,0:T(8,128)(2,1)S(1)} %collective-permute-done.15), channel_id=1, source_target_pairs={{0,28},{4,0},{8,4},{12,8},{16,12},{20,16},{24,20},{28,24},{1,29},{... | collective-permute-start | bytes 24584 | tf_op jit(solution)/shard_map/ppermute | solution.py:22
  410.0 6.3 %collective-permute-start.18 = (bf16[16,256]{1,0:T(8,128)(2,1)S(1)}, bf16[16,256]{1,0:T(8,128)(2,1)S(1)}, u32[]{:S(2)}, u32[]{:S(2)}) collective-permute-start(bf16[16,256]{1,0:T(8,128)(2,1)S(1)} %collective-permute-done.16), channel_id=1, source_target_pairs={{0,4},{4,8},{8,12},{12,16},{16,20},{20,24},{24,28},{28,0},{1,5},{5... | collective-permute-start | bytes 24584 | tf_op jit(solution)/shard_map/ppermute | solution.py:19
  410.0 6.3 %collective-permute-start.19 = (bf16[16,256]{1,0:T(8,128)(2,1)S(1)}, bf16[16,256]{1,0:T(8,128)(2,1)S(1)}, u32[]{:S(2)}, u32[]{:S(2)}) collective-permute-start(bf16[16,256]{1,0:T(8,128)(2,1)S(1)} %collective-permute-done.17), channel_id=1, source_target_pairs={{0,28},{4,0},{8,4},{12,8},{16,12},{20,16},{24,20},{28,24},{1,29},{... | collective-permute-start | bytes 24584 | tf_op jit(solution)/shard_map/ppermute | solution.py:22
  416.3 6.3 %collective-permute-start.20 = (bf16[16,256]{1,0:T(8,128)(2,1)S(1)}, bf16[16,256]{1,0:T(8,128)(2,1)S(1)}, u32[]{:S(2)}, u32[]{:S(2)}) collective-permute-start(bf16[16,256]{1,0:T(8,128)(2,1)S(1)} %collective-permute-done.18), channel_id=1, source_target_pairs={{0,4},{4,8},{8,12},{12,16},{16,20},{20,24},{24,28},{28,0},{1,5},{5... | collective-permute-start | bytes 24584 | tf_op jit(solution)/shard_map/ppermute | solution.py:19
  422.8 84.0 %copy-start.3 = (bf16[1,16,64,128]{3,2,1,0:T(8,128)(2,1)S(1)}, bf16[1,16,64,128]{3,2,1,0:T(8,128)(2,1)}, u32[]{:S(2)}) copy-start(bf16[1,16,64,128]{3,2,1,0:T(8,128)(2,1)} %get-tuple-element.25) | copy-start | bytes 786436
  422.8 84.0 %copy-start.4 = (bf16[1,16,64,128]{3,2,1,0:T(8,128)(2,1)S(1)}, bf16[1,16,64,128]{3,2,1,0:T(8,128)(2,1)}, u32[]{:S(2)}) copy-start(bf16[1,16,64,128]{3,2,1,0:T(8,128)(2,1)} %get-tuple-element.26) | copy-start | bytes 786436
  422.9 84.0 %copy-start.5 = (bf16[1,16,64,128]{3,2,1,0:T(8,128)(2,1)S(1)}, bf16[1,16,64,128]{3,2,1,0:T(8,128)(2,1)}, u32[]{:S(2)}) copy-start(bf16[1,16,64,128]{3,2,1,0:T(8,128)(2,1)} %get-tuple-element.40) | copy-start | bytes 786436
  422.9 84.0 %copy-start.6 = (bf16[1,16,64,128]{3,2,1,0:T(8,128)(2,1)S(1)}, bf16[1,16,64,128]{3,2,1,0:T(8,128)(2,1)}, u32[]{:S(2)}) copy-start(bf16[1,16,64,128]{3,2,1,0:T(8,128)(2,1)} %get-tuple-element.41) | copy-start | bytes 786436
  506.0 6.4 %collective-permute-start.21 = (bf16[16,256]{1,0:T(8,128)(2,1)S(1)}, bf16[16,256]{1,0:T(8,128)(2,1)S(1)}, u32[]{:S(2)}, u32[]{:S(2)}) collective-permute-start(bf16[16,256]{1,0:T(8,128)(2,1)S(1)} %get-tuple-element.18), channel_id=1, source_target_pairs={{0,4},{4,8},{8,12},{12,16},{16,20},{20,24},{24,28},{28,0},{1,5},{5... | collective-permute-start | bytes 24584 | tf_op jit(solution)/shard_map/ppermute | solution.py:19
  507.9 5.3 collective-permute-start.22
  512.4 6.3 %collective-permute-start.23 = (bf16[16,256]{1,0:T(8,128)(2,1)S(1)}, bf16[16,256]{1,0:T(8,128)(2,1)S(1)}, u32[]{:S(2)}, u32[]{:S(2)}) collective-permute-start(bf16[16,256]{1,0:T(8,128)(2,1)S(1)} %collective-permute-done.21), channel_id=1, source_target_pairs={{0,4},{4,8},{8,12},{12,16},{16,20},{20,24},{24,28},{28,0},{1,5},{5... | collective-permute-start | bytes 24584 | tf_op jit(solution)/shard_map/ppermute | solution.py:19
  513.2 6.3 %collective-permute-start.24 = (bf16[16,256]{1,0:T(8,128)(2,1)S(1)}, bf16[16,256]{1,0:T(8,128)(2,1)S(1)}, u32[]{:S(2)}, u32[]{:S(2)}) collective-permute-start(bf16[16,256]{1,0:T(8,128)(2,1)S(1)} %collective-permute-done.22), channel_id=1, source_target_pairs={{0,28},{4,0},{8,4},{12,8},{16,12},{20,16},{24,20},{28,24},{1,29},{... | collective-permute-start | bytes 24584 | tf_op jit(solution)/shard_map/ppermute | solution.py:22
  518.8 6.3 %collective-permute-start.25 = (bf16[16,256]{1,0:T(8,128)(2,1)S(1)}, bf16[16,256]{1,0:T(8,128)(2,1)S(1)}, u32[]{:S(2)}, u32[]{:S(2)}) collective-permute-start(bf16[16,256]{1,0:T(8,128)(2,1)S(1)} %collective-permute-done.23), channel_id=1, source_target_pairs={{0,4},{4,8},{8,12},{12,16},{16,20},{20,24},{24,28},{28,0},{1,5},{5... | collective-permute-start | bytes 24584 | tf_op jit(solution)/shard_map/ppermute | solution.py:19
  519.6 6.3 %collective-permute-start.26 = (bf16[16,256]{1,0:T(8,128)(2,1)S(1)}, bf16[16,256]{1,0:T(8,128)(2,1)S(1)}, u32[]{:S(2)}, u32[]{:S(2)}) collective-permute-start(bf16[16,256]{1,0:T(8,128)(2,1)S(1)} %collective-permute-done.24), channel_id=1, source_target_pairs={{0,28},{4,0},{8,4},{12,8},{16,12},{20,16},{24,20},{28,24},{1,29},{... | collective-permute-start | bytes 24584 | tf_op jit(solution)/shard_map/ppermute | solution.py:22
  525.1 6.3 %collective-permute-start.27 = (bf16[16,256]{1,0:T(8,128)(2,1)S(1)}, bf16[16,256]{1,0:T(8,128)(2,1)S(1)}, u32[]{:S(2)}, u32[]{:S(2)}) collective-permute-start(bf16[16,256]{1,0:T(8,128)(2,1)S(1)} %collective-permute-done.25), channel_id=1, source_target_pairs={{0,4},{4,8},{8,12},{12,16},{16,20},{20,24},{24,28},{28,0},{1,5},{5... | collective-permute-start | bytes 24584 | tf_op jit(solution)/shard_map/ppermute | solution.py:19
  531.5 0.6 copy-start.9
Sparse Core Ops, SparseCore 0:
  165.8 68.1 all-reduce.10
  426.1 68.0 all-reduce.8
